TPU v7x, 32 devices: a whole 2x2x4 slice. The times are simulated.
32 devices in a mesh: fsdp: 2 (over x), ctx: 4 (over y, core), tp: 4 (over z).
Axes of the slice: x: 2, y: 2, z: 4, core: 2. Of those that a mesh axis runs over, the one named last changes fastest.
Arguments:
- inputs: bfloat16 [4, 1024, 2048], P('fsdp', 'ctx'), may hold values from -6 to 6
- prefix: int32 [4], P('fsdp'), may hold values from 102 to 512, as said below
- expert_ids: int32 [4, 1024, 8], P('fsdp', 'ctx'), may hold values from 0 to 15, all different within a row
- norm_gains: bfloat16 [4, 2048], P(None, ('fsdp', 'ctx')), may hold values from 0.5 to 1.5
- qkv_weight: bfloat16 [3, 2048, 2048], P(None, ('fsdp', 'ctx'), 'tp'), may hold values from -0.125 to 0.125
- out_weight: bfloat16 [2048, 2048], P(('fsdp', 'ctx'), 'tp'), may hold values from -1 to 1
- router_weight: bfloat16 [2048, 16], P(('fsdp', 'ctx')), may hold values from -0.0625 to 0.0625
- gate_up_weight: bfloat16 [16, 2, 2048, 1024], P(None, None, ('fsdp', 'ctx'), 'tp'), may hold values from -0.125 to 0.125
- down_weight: bfloat16 [16, 2048, 1024], P(None, ('fsdp', 'ctx'), 'tp'), may hold values from -1.5 to 1.5
- cotangent: bfloat16 [4, 1024, 2048], P('fsdp', 'ctx'), may hold values from -6 to 6
Outputs:
- outputs: bfloat16 [4, 1024, 2048], P('fsdp', 'ctx')
- grad_inputs: bfloat16 [4, 1024, 2048], P('fsdp', 'ctx')
- grad_norm_gains: float32 [4, 2048], P(None, ('fsdp', 'ctx'))
- grad_qkv_weight: float32 [3, 2048, 2048], P(None, ('fsdp', 'ctx'), 'tp')
- grad_out_weight: float32 [2048, 2048], P(('fsdp', 'ctx'), 'tp')
- grad_router_weight: float32 [2048, 16], P(('fsdp', 'ctx'))
- grad_gate_up_weight: float32 [16, 2, 2048, 1024], P(None, None, ('fsdp', 'ctx'), 'tp')
- grad_down_weight: float32 [16, 2048, 1024], P(None, ('fsdp', 'ctx'), 'tp')
Inputs may be any that keep to these rules, and one draw needn't show every extreme that they name: `expert_ids`: each token names 8 different experts. Some sequence has the shortest and some the longest allowed prefix.
All inputs are finite; a program needn't handle non-finite values.
Results may differ from a plain program's by a relative error of at most 0.017.
Values may be sent and summed in bfloat16 or wider, within the bound.
No kernel may reach another device: no remote copies, remote signals or barrier semaphores. Data moves between devices by JAX's collectives and lax.ppermute only.
A program may use at most 384 MiB of HBM per device.

v0:
```python
import jax
import jax.numpy as jnp
from jax import lax
from jax.sharding import PartitionSpec as P

HEAD_DIM = 128
EPSILON = 1e-05
THETA = 10000.0


def rotary_tables(positions, head_width):
    halves = jnp.arange(0, head_width, 2).astype(jnp.float32) / head_width
    inverse = 1.0 / THETA**halves
    angles = positions.astype(jnp.float32)[:, None] * inverse[None, :]
    return (jnp.cos(angles), jnp.sin(angles))


def rotate(values, cosine, sine):
    half = values.shape[-1] // 2
    first = values[..., :half]
    second = values[..., half:]
    cosine = cosine[:, None, :]
    sine = sine[:, None, :]
    return jnp.concatenate([first * cosine - second * sine, second * cosine + first * sine], -1)


def unrotate(grads, cosine, sine):
    half = grads.shape[-1] // 2
    first = grads[..., :half]
    second = grads[..., half:]
    cosine = cosine[:, None, :]
    sine = sine[:, None, :]
    return jnp.concatenate([first * cosine + second * sine, second * cosine - first * sine], -1)


def contract_rows(left, right):
    return lax.dot_general(
        left, right, (((0,), (0,)), ((), ())), preferred_element_type=jnp.float32
    )


def contract_last(left, right):
    return lax.dot_general(
        left, right, (((1,), (1,)), ((), ())), preferred_element_type=jnp.float32
    )


def body(
    inputs,
    prefix,
    expert_ids,
    norm_gains,
    qkv_weight,
    out_weight,
    router_weight,
    gate_up_weight,
    down_weight,
    cotangent,
):
    sequences, local_len, width = inputs.shape
    tokens = sequences * local_len
    full_len = local_len * lax.axis_size("ctx")
    gains_low, qkv_full, out_full = (
        lax.all_gather(norm_gains, ("fsdp", "ctx"), axis=1, tiled=True),
        lax.all_gather(qkv_weight, ("fsdp", "ctx"), axis=1, tiled=True),
        lax.all_gather(out_weight, ("fsdp", "ctx"), axis=0, tiled=True),
    )
    gains = gains_low.astype(jnp.float32)
    local_width = qkv_full.shape[2]
    head_width = HEAD_DIM
    local_heads = local_width // head_width
    head_scale = head_width ** (-0.5)
    column_start = lax.axis_index("tp") * local_width
    query_gain = lax.dynamic_slice_in_dim(gains[2], column_start, local_width)
    key_gain = lax.dynamic_slice_in_dim(gains[3], column_start, local_width)
    residual = inputs.reshape(tokens, width).astype(jnp.float32)
    scale_one = lax.rsqrt(jnp.mean(residual * residual, -1, keepdims=True) + EPSILON)
    normal_one = residual * scale_one
    normed_one = (normal_one * gains[0]).astype(jnp.bfloat16)
    projected = jnp.einsum("td,cde->cte", normed_one, qkv_full, preferred_element_type=jnp.float32)
    query_raw = projected[0]
    key_raw = projected[1]
    value_raw = projected[2]
    query_squares, key_squares = lax.psum(
        (jnp.sum(query_raw * query_raw, -1), jnp.sum(key_raw * key_raw, -1)), "tp"
    )
    query_scale = lax.rsqrt(query_squares / width + EPSILON)[:, None]
    key_scale = lax.rsqrt(key_squares / width + EPSILON)[:, None]
    query_hat = query_raw * query_scale
    key_hat = key_raw * key_scale
    positions = lax.axis_index("ctx") * local_len + jnp.arange(local_len, dtype=jnp.int32)
    cosine, sine = rotary_tables(positions, head_width)
    head_shape = (sequences, local_len, local_heads, head_width)
    queries = rotate((query_hat * query_gain).reshape(head_shape), cosine, sine).astype(
        jnp.bfloat16
    )
    keys_local = rotate((key_hat * key_gain).reshape(head_shape), cosine, sine).astype(jnp.bfloat16)
    values_local = value_raw.reshape(head_shape).astype(jnp.bfloat16)
    all_keys, all_values = (
        lax.all_gather(keys_local, "ctx", axis=1, tiled=True),
        lax.all_gather(values_local, "ctx", axis=1, tiled=True),
    )
    key_places = jnp.arange(full_len, dtype=jnp.int32)
    visible = (key_places[None, None, :] <= positions[None, :, None]) | (
        key_places[None, None, :] < prefix[:, None, None]
    )
    visible = visible[:, None]
    scores = (
        jnp.einsum("sqhd,skhd->shqk", queries, all_keys, preferred_element_type=jnp.float32)
        * head_scale
    )
    masked = jnp.where(visible, scores, -1e30)
    maxima = jnp.max(masked, -1, keepdims=True)
    expo = jnp.exp(masked - maxima)
    totals = jnp.sum(expo, -1, keepdims=True)
    probs = expo / totals
    log_total = maxima + jnp.log(totals)
    heads_out = jnp.einsum(
        "shqk,skhd->sqhd",
        probs.astype(jnp.bfloat16),
        all_values,
        preferred_element_type=jnp.float32,
    )
    heads_out = heads_out.astype(jnp.bfloat16).reshape(tokens, local_width)
    attn_total = lax.psum(contract_last(heads_out, out_full), "tp")
    mid = residual + attn_total
    scale_two = lax.rsqrt(jnp.mean(mid * mid, -1, keepdims=True) + EPSILON)
    normal_two = mid * scale_two
    normed_two = (normal_two * gains[1]).astype(jnp.bfloat16)
    gate_up_full, down_full, router_full = (
        lax.all_gather(gate_up_weight, ("fsdp", "ctx"), axis=2, tiled=True),
        lax.all_gather(down_weight, ("fsdp", "ctx"), axis=1, tiled=True),
        lax.all_gather(router_weight, ("fsdp", "ctx"), axis=0, tiled=True),
    )
    expert_count = router_full.shape[1]
    logits = jnp.dot(normed_two, router_full, preferred_element_type=jnp.float32)
    router_probs = jax.nn.softmax(logits, -1)
    chosen = jnp.sum(
        (
            expert_ids.reshape(tokens, -1)[:, :, None]
            == jnp.arange(expert_count, dtype=jnp.int32)[None, None, :]
        ).astype(jnp.float32),
        1,
    )
    gates = router_probs * chosen

    def expert_forward(carry, entries):
        pair_weights, down_one, gate_one = entries
        activations = jnp.einsum(
            "td,cdf->ctf", normed_two, pair_weights, preferred_element_type=jnp.float32
        )
        hidden = (gate_one[:, None] * jax.nn.silu(activations[0]) * activations[1]).astype(
            jnp.bfloat16
        )
        return (carry + contract_last(hidden, down_one), activations)

    moe_part, kept_activations = lax.scan(
        expert_forward, jnp.zeros((tokens, width), jnp.float32), (gate_up_full, down_full, gates.T)
    )
    moe_total = lax.psum(moe_part.astype(jnp.bfloat16), "tp").astype(jnp.float32)
    outputs = (mid + moe_total).astype(jnp.bfloat16).reshape(inputs.shape)
    grad_out = cotangent.reshape(tokens, width)
    grad_float = grad_out.astype(jnp.float32)
    gate_up_back, down_back, router_back = (
        lax.all_gather(gate_up_weight, ("fsdp", "ctx"), axis=2, tiled=True),
        lax.all_gather(down_weight, ("fsdp", "ctx"), axis=1, tiled=True),
        lax.all_gather(router_weight, ("fsdp", "ctx"), axis=0, tiled=True),
    )

    def expert_backward(carry, entries):
        pair_weights, down_one, gate_one, activations = entries
        grad_hidden = jnp.dot(grad_out, down_one, preferred_element_type=jnp.float32)
        sigma = jax.nn.sigmoid(activations[0])
        swish = jax.nn.silu(activations[0])
        hidden = (gate_one[:, None] * swish * activations[1]).astype(jnp.bfloat16)
        grad_down = contract_rows(grad_out, hidden)
        grad_gate = jnp.sum(grad_hidden * swish * activations[1], -1)
        grad_inner = grad_hidden * gate_one[:, None]
        grad_act_gate = grad_inner * activations[1] * sigma * (1.0 + activations[0] * (1.0 - sigma))
        grad_act_up = grad_inner * swish
        grad_acts = jnp.stack([grad_act_gate, grad_act_up]).astype(jnp.bfloat16)
        grad_pair = jnp.einsum(
            "td,ctf->cdf", normed_two, grad_acts, preferred_element_type=jnp.float32
        )
        carry = carry + jnp.einsum(
            "ctf,cdf->td", grad_acts, pair_weights, preferred_element_type=jnp.float32
        )
        return (carry, (grad_pair, grad_down, grad_gate))

    back_inputs = (gate_up_back, down_back, gates.T, kept_activations)
    zero_rows = jnp.zeros((tokens, width), jnp.float32)
    expert_part, (grad_gate_up, grad_down_all, grad_gates) = lax.scan(
        expert_backward, zero_rows, back_inputs
    )
    expert_grad_norm, gate_grads = lax.psum((expert_part, grad_gates.T), "tp")
    masked_grads = gate_grads * chosen
    grad_logits = (
        router_probs * (masked_grads - jnp.sum(router_probs * masked_grads, -1, keepdims=True))
    ).astype(jnp.bfloat16)
    grad_router = contract_rows(normed_two, grad_logits)
    grad_normed_two = expert_grad_norm + contract_last(grad_logits, router_back)
    owned_gate_up, owned_down, owned_router = (
        lax.psum_scatter(grad_gate_up, ("fsdp", "ctx"), scatter_dimension=2, tiled=True),
        lax.psum_scatter(grad_down_all, ("fsdp", "ctx"), scatter_dimension=1, tiled=True),
        lax.psum_scatter(grad_router, ("fsdp", "ctx"), scatter_dimension=0, tiled=True),
    )
    weighted_two = grad_normed_two * gains[1]
    grad_mid = grad_float + scale_two * (
        weighted_two - normal_two * jnp.mean(weighted_two * normal_two, -1, keepdims=True)
    )
    gain_two_grad = jnp.sum(grad_normed_two * normal_two, 0)
    grad_mid_low = grad_mid.astype(jnp.bfloat16)
    grad_out_weight = contract_rows(grad_mid_low, heads_out)
    grad_heads = (
        jnp.dot(grad_mid_low, out_full, preferred_element_type=jnp.float32)
        .astype(jnp.bfloat16)
        .reshape(head_shape)
    )
    scores_again = (
        jnp.einsum("sqhd,skhd->shqk", queries, all_keys, preferred_element_type=jnp.float32)
        * head_scale
    )
    probs_again = jnp.exp(jnp.where(visible, scores_again, -1e30) - log_total)
    grad_probs = jnp.einsum(
        "sqhd,skhd->shqk", grad_heads, all_values, preferred_element_type=jnp.float32
    )
    inner_sums = jnp.sum(probs_again * grad_probs, -1, keepdims=True)
    grad_scores = (probs_again * (grad_probs - inner_sums)).astype(jnp.bfloat16)
    grad_queries = (
        jnp.einsum("shqk,skhd->sqhd", grad_scores, all_keys, preferred_element_type=jnp.float32)
        * head_scale
    )
    grad_keys_all = (
        jnp.einsum("shqk,sqhd->skhd", grad_scores, queries, preferred_element_type=jnp.float32)
        * head_scale
    )
    grad_values_all = jnp.einsum(
        "shqk,sqhd->skhd",
        probs_again.astype(jnp.bfloat16),
        grad_heads,
        preferred_element_type=jnp.float32,
    )
    grad_keys, grad_values = (
        lax.psum_scatter(grad_keys_all, "ctx", scatter_dimension=1, tiled=True),
        lax.psum_scatter(grad_values_all, "ctx", scatter_dimension=1, tiled=True),
    )
    grad_query_hat = unrotate(grad_queries, cosine, sine).reshape(tokens, local_width)
    grad_key_hat = unrotate(grad_keys, cosine, sine).reshape(tokens, local_width)
    weighted_query = grad_query_hat * query_gain
    weighted_key = grad_key_hat * key_gain
    query_inner, key_inner = lax.psum(
        (jnp.sum(weighted_query * query_hat, -1), jnp.sum(weighted_key * key_hat, -1)), "tp"
    )
    grad_query_raw = (
        query_scale * (weighted_query - query_hat * (query_inner / width)[:, None])
    ).astype(jnp.bfloat16)
    grad_key_raw = (key_scale * (weighted_key - key_hat * (key_inner / width)[:, None])).astype(
        jnp.bfloat16
    )
    grad_value_raw = grad_values.reshape(tokens, local_width).astype(jnp.bfloat16)
    grad_projected = jnp.stack([grad_query_raw, grad_key_raw, grad_value_raw])
    grad_qkv = jnp.einsum(
        "td,cte->cde", normed_one, grad_projected, preferred_element_type=jnp.float32
    )
    grad_normed_part = jnp.einsum(
        "cte,cde->td", grad_projected, qkv_full, preferred_element_type=jnp.float32
    )
    local_gain_grads = jnp.stack(
        [jnp.sum(grad_query_hat * query_hat, 0), jnp.sum(grad_key_hat * key_hat, 0)]
    )
    placed_gains = lax.dynamic_update_slice_in_dim(
        jnp.zeros((2, width), jnp.float32), local_gain_grads, column_start, 1
    )
    grad_normed_one, qk_gain_grads = lax.psum((grad_normed_part, placed_gains), "tp")
    weighted_one = grad_normed_one * gains[0]
    grad_input = grad_mid + scale_one * (
        weighted_one - normal_one * jnp.mean(weighted_one * normal_one, -1, keepdims=True)
    )
    gain_one_grad = jnp.sum(grad_normed_one * normal_one, 0)
    grad_gains = jnp.stack([gain_one_grad, gain_two_grad, qk_gain_grads[0], qk_gain_grads[1]])
    owned_gains, owned_qkv, owned_out = (
        lax.psum_scatter(grad_gains, ("fsdp", "ctx"), scatter_dimension=1, tiled=True),
        lax.psum_scatter(grad_qkv, ("fsdp", "ctx"), scatter_dimension=1, tiled=True),
        lax.psum_scatter(grad_out_weight, ("fsdp", "ctx"), scatter_dimension=0, tiled=True),
    )
    return (
        outputs,
        grad_input.astype(jnp.bfloat16).reshape(inputs.shape),
        owned_gains,
        owned_qkv,
        owned_out,
        owned_router,
        owned_gate_up,
        owned_down,
    )


def solution(mesh):
    return jax.shard_map(
        body,
        mesh=mesh,
        in_specs=(
            P("fsdp", "ctx", None),
            P("fsdp"),
            P("fsdp", "ctx", None),
            P(None, ("fsdp", "ctx")),
            P(None, ("fsdp", "ctx"), "tp"),
            P(("fsdp", "ctx"), "tp"),
            P(("fsdp", "ctx"), None),
            P(None, None, ("fsdp", "ctx"), "tp"),
            P(None, ("fsdp", "ctx"), "tp"),
            P("fsdp", "ctx", None),
        ),
        out_specs=(
            P("fsdp", "ctx", None),
            P("fsdp", "ctx", None),
            P(None, ("fsdp", "ctx")),
            P(None, ("fsdp", "ctx"), "tp"),
            P(("fsdp", "ctx"), "tp"),
            P(("fsdp", "ctx"), None),
            P(None, None, ("fsdp", "ctx"), "tp"),
            P(None, ("fsdp", "ctx"), "tp"),
        ),
        check_vma=False,
    )
```

profile of v0, /device:TPU:0, one launch (start us, length us, event | category | flops | bytes accessed | tf_op | source)
XLA Modules:
  0.0 2617.0 jit_solution(943007271589671076)
XLA Ops:
  11.9 10.4 all_gather.27
  24.7 35.1 %all-gather.7.cloned.1.call-done = bf16[3,2048,512]{1,2,0:T(8,128)(2,1)} async-done(((bf16[3,256,512]{1,2,0:T(8,128)(2,1)}), bf16[3,2048,512]{1,2,0:T(8,128)(2,1)}) %all-gather.7.cloned.1.call-update) | async-done | bytes 6291472 | tf_op jit(solution)/shard_map/all_gather | solution.py:65
  59.9 6.2 fusion.52
  69.0 11.7 all-reduce.1
  101.0 11.4 all-gather.11.cloned.1.call-done
  121.4 16.0 all-gather.9.cloned.1.call-done
  137.4 5.8 fusion.57
  143.6 23.5 all-gather.13.cloned.1.call-done
  173.5 9.2 all_gather.32
  182.7 144.4 %all-reduce.7.cloned.1.call-done = f32[512,2048]{1,0:T(8,128)} async-done(((f32[512,2048]{1,0:T(8,128)}), f32[512,2048]{1,0:T(8,128)}) %all-reduce.7.cloned.1.call-update) | async-done | bytes 4194320 | tf_op jit(solution)/shard_map/psum | solution.py:125
  332.0 86.0 %all-gather.17.cloned.1.call-done = bf16[16,2048,256]{2,1,0:T(8,128)(2,1)} async-done(((bf16[16,256,256]{2,1,0:T(8,128)(2,1)}), bf16[16,2048,256]{2,1,0:T(8,128)(2,1)}) %all-gather.17.cloned.1.call-update) | async-done | bytes 16777232 | tf_op jit(solution)/shard_map/all_gather | solution.py:132
  418.0 162.9 %all-gather.15.cloned.1.call-done = bf16[16,2,2048,256]{3,2,1,0:T(8,128)(2,1)} async-done(((bf16[16,2,256,256]{3,2,1,0:T(8,128)(2,1)}), bf16[16,2,2048,256]{3,2,1,0:T(8,128)(2,1)}) %all-gather.15.cloned.1.call-update) | async-done | bytes 33554448 | tf_op jit(solution)/shard_map/all_gather | solution.py:131
  580.9 145.9 %while.30 = (s32[]{:T(128)}, f32[512,2048]{1,0:T(8,128)}, f32[16,2,512,256]{2,3,1,0:T(8,128)}, f32[16,512]{1,0:T(8,128)S(1)}, bf16[16,2,2048,256]{3,2,1,0:T(8,12...) while((s32[]{:T(128)}, f32[512,2048]{1,0:T(8,128)}, ...), condition=%wide.region_13.14_spmd.clone, body=%wide.region_12.13_spmd.clone.sunk | while | flops 1613627392 | bytes 50338988 | solution.py:157
  726.8 503.8 %while.31 = (s32[]{:T(128)}, f32[512,2048]{1,0:T(8,128)}, f32[16,2,2048,256]{3,2,1,0:T(8,128)}, f32[16,2048,256]{2,1,0:T(8,128)}, f32[16,512]{1,0:T(8,128)S(1)},...) while((s32[]{:T(128)}, f32[512,2048]{1,0:T(8,128)}, ...), condition=%wide.region_17.18_spmd.clone, body=%wide.region_15.17_spmd.clone.sunk | while | flops 3226992128 | bytes 86523664 | solution.py:192
  767.0 6.2 bitcast_add_fusion.4
  798.6 6.2 bitcast_add_fusion.4
  830.1 6.2 bitcast_add_fusion.4
  861.7 6.2 bitcast_add_fusion.4
  893.3 6.2 bitcast_add_fusion.4
  924.8 6.2 bitcast_add_fusion.4
  956.4 6.2 bitcast_add_fusion.4
  988.0 6.2 bitcast_add_fusion.4
  1019.5 6.2 bitcast_add_fusion.4
  1051.1 6.2 bitcast_add_fusion.4
  1082.6 6.2 bitcast_add_fusion.4
  1114.2 6.2 bitcast_add_fusion.4
  1145.8 6.2 bitcast_add_fusion.4
  1177.3 6.2 bitcast_add_fusion.4
  1208.9 6.2 bitcast_add_fusion.4
  1234.6 20.3 psum.75
  1255.0 131.8 %all-reduce.11.cloned.1.call-done = f32[512,2048]{1,0:T(8,128)} async-done(((f32[512,2048]{1,0:T(8,128)}), f32[512,2048]{1,0:T(8,128)}) %all-reduce.11.cloned.1.call-update) | async-done | bytes 4194320 | tf_op jit(solution)/shard_map/psum | solution.py:195
  1386.7 6.7 multiply_reduce_fusion.2
  1393.4 81.8 %all-reduce.9.cloned.1.call-done = bf16[512,2048]{1,0:T(8,128)(2,1)} async-done(((bf16[512,2048]{1,0:T(8,128)(2,1)}), bf16[512,2048]{1,0:T(8,128)(2,1)}) %all-reduce.9.cloned.1.call-update) | async-done | bytes 2097168 | tf_op jit(solution)/shard_map/psum | solution.py:160
  1475.2 6.7 multiply_add_fusion
  1485.6 7.0 fusion.46
  1514.6 21.7 reduce-scatter.13.cloned.1.call-done
  1541.1 42.3 %reduce-scatter.11.cloned.1.call-done = f32[2,256,4,128]{3,1,2,0:T(8,128)} async-done(((f32[2,1024,4,128]{3,1,2,0:T(8,128)}), f32[2,256,4,128]{3,1,2,0:T(8,128)}) %reduce-scatter.11.cloned.1.call-update) | async-done | bytes 1048592 | tf_op jit(solution)/shard_map/reduce_scatter | solution.py:244
  1601.3 19.0 all-reduce
  1623.6 7.8 convolution_bitcast_fusion.4
  1631.5 152.3 %all-reduce.13.cloned.1.call-done = f32[512,2048]{1,0:T(8,128)} async-done(((f32[512,2048]{1,0:T(8,128)}), f32[512,2048]{1,0:T(8,128)}) %all-reduce.13.cloned.1.call-update) | async-done | bytes 4194320 | tf_op jit(solution)/shard_map/psum | solution.py:274
  1789.7 9.8 convolution_bitcast_fusion.3
  1808.4 5.9 fusion.41
  1814.3 10.1 reduce-scatter.25.cloned.1.call-done
  1826.0 94.2 %reduce-scatter.15.cloned.1.call-done = f32[3,256,512]{1,2,0:T(8,128)} async-done(((f32[3,2048,512]{1,2,0:T(8,128)}), f32[3,256,512]{1,2,0:T(8,128)}) %reduce-scatter.15.cloned.1.call-update) | async-done | bytes 1572880 | tf_op jit(solution)/shard_map/reduce_scatter | solution.py:283
  1923.2 33.8 %reduce-scatter.19.cloned.1.call-done = f32[256,16]{0,1:T(8,128)} async-done(((f32[2048,16]{0,1:T(8,128)}), f32[256,16]{0,1:T(8,128)}) %reduce-scatter.19.cloned.1.call-update) | async-done | bytes 16400 | tf_op jit(solution)/shard_map/reduce_scatter | solution.py:205
  1957.0 55.5 %reduce-scatter.17.cloned.1.call-done = f32[256,512]{1,0:T(8,128)} async-done(((f32[2048,512]{1,0:T(8,128)}), f32[256,512]{1,0:T(8,128)}) %reduce-scatter.17.cloned.1.call-update) | async-done | bytes 524304 | tf_op jit(solution)/shard_map/reduce_scatter | solution.py:284
  2012.5 209.3 %reduce-scatter.23.cloned.1.call-done = f32[16,256,256]{2,1,0:T(8,128)} async-done(((f32[16,2048,256]{2,1,0:T(8,128)}), f32[16,256,256]{2,1,0:T(8,128)}) %reduce-scatter.23.cloned.1.call-update) | async-done | bytes 4194320 | tf_op jit(solution)/shard_map/reduce_scatter | solution.py:204
  2221.8 388.2 %reduce-scatter.21.cloned.1.call-done = f32[16,2,256,256]{3,2,1,0:T(8,128)} async-done(((f32[16,2,2048,256]{3,2,1,0:T(8,128)}), f32[16,2,256,256]{3,2,1,0:T(8,128)}) %reduce-scatter.21.cloned.1.call-update) | async-done | bytes 8388624 | tf_op jit(solution)/shard_map/reduce_scatter | solution.py:203
  (548 shorter events, 681.8 us)
Async XLA Ops:
  7.2 15.7 copy-start.8
  7.2 4.7 copy-start.42
  7.2 52.7 %all-gather.7.cloned.1.call-start = ((), (), s32[]{:S(2)}) async-start(), calls=%async_computation.8 | async-start | bytes 7077888 | tf_op jit(solution)/shard_map/all_gather | solution.py:65
  9.7 102.7 %all-gather.11.cloned.1.call-start = ((), (), s32[]{:S(2)}) async-start(), calls=%async_computation.10 | async-start | bytes 2621440 | tf_op jit(solution)/shard_map/all_gather | solution.py:100
  11.8 54.3 %copy-start.30 = (f32[1,2,2,128]{3,1,2,0:T(2,128)}, f32[1,2,2,128]{3,1,2,0:T(2,128)S(1)}, u32[]{:S(2)}) copy-start(f32[1,2,2,128]{3,1,2,0:T(2,128)S(1)} %copy.139) | copy-start | bytes 6148
  22.3 37.6 %copy-start.28 = (f32[1,2048]{1,0:T(1,128)}, f32[1,2048]{1,0:T(1,128)S(1)}, u32[]{:S(2)}) copy-start(f32[1,2048]{1,0:T(1,128)S(1)} %get-tuple-element.315) | copy-start | bytes 24580
  22.3 66.6 %copy-start.38 = (f32[1,512]{1,0:T(1,128)}, f32[1,512]{1,0:T(1,128)S(1)}, u32[]{:S(2)}) copy-start(f32[1,512]{1,0:T(1,128)S(1)} %get-tuple-element.326) | copy-start | bytes 6148
  22.3 68.0 %copy-start.36 = (f32[1,512]{1,0:T(1,128)}, f32[1,512]{1,0:T(1,128)S(1)}, u32[]{:S(2)}) copy-start(f32[1,512]{1,0:T(1,128)S(1)} %get-tuple-element.325) | copy-start | bytes 6148
  22.9 67.7 %copy-start.19 = (f32[256,64]{1,0:T(8,128)}, f32[256,64]{1,0:T(8,128)S(1)}, u32[]{:S(2)}) copy-start(f32[256,64]{1,0:T(8,128)S(1)} %get-tuple-element.316) | copy-start | bytes 196612
  22.9 67.7 %copy-start.21 = (f32[256,64]{1,0:T(8,128)}, f32[256,64]{1,0:T(8,128)S(1)}, u32[]{:S(2)}) copy-start(f32[256,64]{1,0:T(8,128)S(1)} %get-tuple-element.317) | copy-start | bytes 196612
  80.7 8.2 copy-start.32
  80.7 8.2 copy-start.34
  91.3 24.9 copy-start.14
  91.3 24.9 copy-start.16
  91.3 8.4 copy-start.43
  92.4 45.0 %all-gather.9.cloned.1.call-start = ((), (), s32[]{:S(2)}) async-start(), calls=%async_computation.9 | async-start | bytes 2621440 | tf_op jit(solution)/shard_map/all_gather | solution.py:101
  98.5 68.6 %all-gather.13.cloned.1.call-start = ((), (), s32[]{:S(2)}) async-start(), calls=%async_computation.11 | async-start | bytes 2359296 | tf_op jit(solution)/shard_map/all_gather | solution.py:66
  99.1 228.1 %all-reduce.7.cloned.1.call-start = ((), (), s32[]{:S(2)}) async-start(), calls=%async_computation.12 | async-start | bytes 8388608 | tf_op jit(solution)/shard_map/psum | solution.py:125
  143.6 28.5 %copy-start.12 = (bf16[2,256,4,128]{3,2,1,0:T(4,128)(2,1)}, bf16[2,256,4,128]{3,2,1,0:T(4,128)(2,1)S(1)}, u32[]{:S(2)}) copy-start(bf16[2,256,4,128]{3,2,1,0:T(4,128)(2,1)S(1)} %copy.90) | copy-start | bytes 1572868
  172.0 10.7 copy-start.40
  172.1 245.9 %all-gather.17.cloned.1.call-start = ((), (), s32[]{:S(2)}) async-start(), calls=%async_computation.14 | async-start | bytes 18874368 | tf_op jit(solution)/shard_map/all_gather | solution.py:132
  172.6 408.2 %all-gather.15.cloned.1.call-start = ((), (), s32[]{:S(2)}) async-start(), calls=%async_computation.13 | async-start | bytes 37748736 | tf_op jit(solution)/shard_map/all_gather | solution.py:131
  173.4 1213.3 %all-reduce.11.cloned.1.call-start = ((), (), s32[]{:S(2)}) async-start(), calls=%async_computation.16 | async-start | bytes 8388608 | tf_op jit(solution)/shard_map/psum | solution.py:195
  653.8 4.1 copy-start.2
  690.3 4.1 copy-start.2
  1230.6 244.6 %all-reduce.9.cloned.1.call-start = ((), (), s32[]{:S(2)}) async-start(), calls=%async_computation.15 | async-start | bytes 4194304 | tf_op jit(solution)/shard_map/psum | solution.py:160
  1234.5 301.7 %reduce-scatter.13.cloned.1.call-start = ((), (), s32[]{:S(2)}) async-start(), calls=%async_computation.18 | async-start | bytes 5242880 | tf_op jit(solution)/shard_map/reduce_scatter | solution.py:245
  1475.2 8.7 copy-start.18
  1492.6 90.7 %reduce-scatter.11.cloned.1.call-start = ((), (), s32[]{:S(2)}) async-start(), calls=%async_computation.17 | async-start | bytes 5242880 | tf_op jit(solution)/shard_map/reduce_scatter | solution.py:244
  1498.2 7.7 copy-start.15
  1498.2 7.7 copy-start.17
  1509.8 73.5 %copy-start.20 = (f32[256,64]{1,0:T(8,128)S(1)}, f32[256,64]{1,0:T(8,128)}, u32[]{:S(2)}) copy-start(f32[256,64]{1,0:T(8,128)} %copy-done.19) | copy-start | bytes 196612
  1509.8 73.5 %copy-start.22 = (f32[256,64]{1,0:T(8,128)S(1)}, f32[256,64]{1,0:T(8,128)}, u32[]{:S(2)}) copy-start(f32[256,64]{1,0:T(8,128)} %copy-done.21) | copy-start | bytes 196612
  1509.8 274.0 %all-reduce.13.cloned.1.call-start = ((), (), s32[]{:S(2)}) async-start(), calls=%async_computation.19 | async-start | bytes 8388608 | tf_op jit(solution)/shard_map/psum | solution.py:274
  1590.6 8.2 copy-start.33
  1590.6 8.2 copy-start.35
  1590.7 8.2 copy-start.37
  1590.7 8.2 copy-start.39
  1631.4 152.4 %copy-start.29 = (f32[1,2048]{1,0:T(1,128)S(1)}, f32[1,2048]{1,0:T(1,128)}, u32[]{:S(2)}) copy-start(f32[1,2048]{1,0:T(1,128)} %copy-done.28) | copy-start | bytes 24580
  1631.4 152.4 %copy-start.31 = (f32[1,2,2,128]{3,1,2,0:T(2,128)S(1)}, f32[1,2,2,128]{3,1,2,0:T(2,128)}, u32[]{:S(2)}) copy-start(f32[1,2,2,128]{3,1,2,0:T(2,128)} %copy-done.30) | copy-start | bytes 6148
  1631.4 158.3 %copy-start.24 = (bf16[1,512,512]{1,2,0:T(8,128)(2,1)S(1)}, bf16[1,512,512]{1,2,0:T(8,128)(2,1)}, u32[]{:S(2)}) copy-start(bf16[1,512,512]{1,2,0:T(8,128)(2,1)} %copy-done.23) | copy-start | bytes 1572868
  1631.4 158.3 %copy-start.26 = (bf16[1,512,512]{1,2,0:T(8,128)(2,1)S(1)}, bf16[1,512,512]{1,2,0:T(8,128)(2,1)}, u32[]{:S(2)}) copy-start(bf16[1,512,512]{1,2,0:T(8,128)(2,1)} %copy-done.25) | copy-start | bytes 1572868
  1631.5 193.0 %reduce-scatter.25.cloned.1.call-start = ((), (), s32[]{:S(2)}) async-start(), calls=%async_computation.25 | async-start | bytes 1179648
  1789.2 131.0 %reduce-scatter.15.cloned.1.call-start = ((), (), s32[]{:S(2)}) async-start(), calls=%async_computation.20 | async-start | bytes 14155776 | tf_op jit(solution)/shard_map/reduce_scatter | solution.py:283
  1799.5 157.5 %reduce-scatter.19.cloned.1.call-start = ((), (), s32[]{:S(2)}) async-start(), calls=%async_computation.22 | async-start | bytes 147456 | tf_op jit(solution)/shard_map/reduce_scatter | solution.py:205
  1800.6 211.9 %reduce-scatter.17.cloned.1.call-start = ((), (), s32[]{:S(2)}) async-start(), calls=%async_computation.21 | async-start | bytes 4718592 | tf_op jit(solution)/shard_map/reduce_scatter | solution.py:284
  1806.2 415.6 %reduce-scatter.23.cloned.1.call-start = ((), (), s32[]{:S(2)}) async-start(), calls=%async_computation.24 | async-start | bytes 37748736 | tf_op jit(solution)/shard_map/reduce_scatter | solution.py:204
  1806.8 803.2 %reduce-scatter.21.cloned.1.call-start = ((), (), s32[]{:S(2)}) async-start(), calls=%async_computation.23 | async-start | bytes 75497472 | tf_op jit(solution)/shard_map/reduce_scatter | solution.py:203
  (89 other events, 257.4 us)
Sparse Core Ops, SparseCore 0:
  10.5 49.3 all-gather.6
  92.6 19.8 all-gather.10
  114.6 22.8 all-gather.8
  139.2 27.8 all-gather.12
  172.2 154.9 all-reduce.6
  329.1 88.8 all-gather.16
  420.0 160.7 all-gather.14
  1230.7 155.9 all-reduce.10
  1389.7 85.5 all-reduce.8
  1492.8 43.4 reduce-scatter.12
  1538.8 44.5 reduce-scatter.10
  1631.6 152.2 all-reduce.12
  1789.3 35.0 reduce-scatter.24
  1827.8 92.3 reduce-scatter.14
  1923.6 33.3 reduce-scatter.18
  1961.1 51.3 reduce-scatter.16
  2016.5 205.2 reduce-scatter.22
  2226.2 383.7 reduce-scatter.20
where the time goes:
time: 2630 us; the launch traced here: 2620 us
  waiting for transfers between devices  1700 us (65%)
  matrix products  489 us (19%)
  local copies, waits for them, and re-layouts  282 us (11%)
  blocking collectives  70.5 us (3%)
  other arithmetic  54.7 us (2%)
    reduce_scatter x1, waiting for transfers between devices, body(): lax.psum_scatter(grad_gate_up, ('fsdp', 'ctx'), scatter_dimension=2, tile...  388 us
    reduce_scatter x1, waiting for transfers between devices, body(): lax.psum_scatter(grad_down_all, ('fsdp', 'ctx'), scatter_dimension=1, til...  209 us
    dynamic_update_slice x80, local copies, waits for them, and re-layouts, body(): lax.scan(expert_backward, zero_rows, back_inputs)  176 us
    all_gather x1, waiting for transfers between devices, body(): lax.all_gather(gate_up_weight, ('fsdp', 'ctx'), axis=2, tiled=True)  163 us
    psum x1, waiting for transfers between devices, body(): lax.psum((grad_normed_part, placed_gains), 'tp')  152 us
    psum x1, waiting for transfers between devices, body(): attn_total = lax.psum(contract_last(heads_out, out_full), 'tp')  144 us
    psum x1, waiting for transfers between devices, body(): expert_grad_norm, gate_grads = lax.psum((expert_part, grad_gates.T), 'tp')  132 us
    dot_general x16, matrix products, expert_backward(): jnp.einsum('ctf,cdf->td', grad_acts, pair_weights, preferred_element_type...  97.3 us
  transfers between devices with their start and end apart: 18, of which 18 were waited for; matrix products, arithmetic and copies ran while one was open for 3% of the time, Pallas kernels for 0%

commit v1 on v0

--- a/solution.py
+++ b/solution.py
@@ -122,7 +122,7 @@
         preferred_element_type=jnp.float32,
     )
     heads_out = heads_out.astype(jnp.bfloat16).reshape(tokens, local_width)
-    attn_total = lax.psum(contract_last(heads_out, out_full), "tp")
+    attn_total = jnp.sum(lax.all_gather(contract_last(heads_out, out_full), "tp"), axis=0)
     mid = residual + attn_total
     scale_two = lax.rsqrt(jnp.mean(mid * mid, -1, keepdims=True) + EPSILON)
     normal_two = mid * scale_two

time: 2630 us -> 2760 us (1.049)
  waiting for transfers between devices: 1700 us -> 1820 us
    all_gather x0 -> x1, waiting for transfers between devices: none -> 276 us  [body(): lax.all_gather(contract_last(heads_out, out_full), 'tp')]
    psum x1 -> x0, waiting for transfers between devices: 144 us -> none  [body(): attn_total = lax.psum(contract_last(heads_out, out_full), 'tp')]
  transfers between devices with their start and end apart: 18 -> 18, of which waited for: 18 -> 18; matrix products, arithmetic and copies ran while one was open for 3% -> 4% of each run, Pallas kernels for 0% -> 0%
where the time goes in v1:
time: 2760 us; the launch traced here: 2750 us
  waiting for transfers between devices  1820 us (66%)
  matrix products  490 us (18%)
  local copies, waits for them, and re-layouts  285 us (10%)
  blocking collectives  71.6 us (3%)
  other arithmetic  66.5 us (2%)
    reduce_scatter x1, waiting for transfers between devices, body(): lax.psum_scatter(grad_gate_up, ('fsdp', 'ctx'), scatter_dimension=2, tile...  388 us
    all_gather x1, waiting for transfers between devices, body(): lax.all_gather(contract_last(heads_out, out_full), 'tp')  276 us
    reduce_scatter x1, waiting for transfers between devices, body(): lax.psum_scatter(grad_down_all, ('fsdp', 'ctx'), scatter_dimension=1, til...  210 us
    dynamic_update_slice x80, local copies, waits for them, and re-layouts, body(): lax.scan(expert_backward, zero_rows, back_inputs)  177 us
    all_gather x1, waiting for transfers between devices, body(): lax.all_gather(gate_up_weight, ('fsdp', 'ctx'), axis=2, tiled=True)  163 us
    psum x1, waiting for transfers between devices, body(): lax.psum((grad_normed_part, placed_gains), 'tp')  152 us
    psum x1, waiting for transfers between devices, body(): expert_grad_norm, gate_grads = lax.psum((expert_part, grad_gates.T), 'tp')  131 us
    dot_general x16, matrix products, expert_backward(): jnp.einsum('ctf,cdf->td', grad_acts, pair_weights, preferred_element_type...  97.3 us
  transfers between devices with their start and end apart: 18, of which 18 were waited for; matrix products, arithmetic and copies ran while one was open for 4% of the time, Pallas kernels for 0%

profile of v1, /device:TPU:0, one launch (start us, length us, event | category | flops | bytes accessed | tf_op | source)
XLA Modules:
  0.0 2752.8 jit_solution(18016220888486008717)
XLA Ops:
  11.9 10.4 all_gather.33
  24.7 35.1 %all-gather.9.cloned.1.call-done = bf16[3,2048,512]{1,2,0:T(8,128)(2,1)} async-done(((bf16[3,256,512]{1,2,0:T(8,128)(2,1)}), bf16[3,2048,512]{1,2,0:T(8,128)(2,1)}) %all-gather.9.cloned.1.call-update) | async-done | bytes 6291472 | tf_op jit(solution)/shard_map/all_gather | solution.py:65
  59.9 6.2 fusion.54
  69.0 11.7 all-reduce.1
  100.6 11.8 all-gather.13.cloned.1.call-done
  121.4 16.0 all-gather.11.cloned.1.call-done
  143.5 23.5 all-gather.15.cloned.1.call-done
  173.5 9.0 all_gather.40
  182.5 276.4 %all-gather.21.cloned.1.call-done = f32[2048,2048]{1,0:T(8,128)} async-done(((f32[512,2048]{1,0:T(8,128)}), f32[2048,2048]{1,0:T(8,128)}) %all-gather.21.cloned.1.call-update) | async-done | bytes 16777232 | tf_op jit(solution)/shard_map/all_gather | solution.py:125
  458.9 10.2 reduce_sum.177
  475.1 73.6 %all-gather.19.cloned.1.call-done = bf16[16,2048,256]{2,1,0:T(8,128)(2,1)} async-done(((bf16[16,256,256]{2,1,0:T(8,128)(2,1)}), bf16[16,2048,256]{2,1,0:T(8,128)(2,1)}) %all-gather.19.cloned.1.call-update) | async-done | bytes 16777232 | tf_op jit(solution)/shard_map/all_gather | solution.py:132
  548.8 162.7 %all-gather.17.cloned.1.call-done = bf16[16,2,2048,256]{3,2,1,0:T(8,128)(2,1)} async-done(((bf16[16,2,256,256]{3,2,1,0:T(8,128)(2,1)}), bf16[16,2,2048,256]{3,2,1,0:T(8,128)(2,1)}) %all-gather.17.cloned.1.call-update) | async-done | bytes 33554448 | tf_op jit(solution)/shard_map/all_gather | solution.py:131
  711.5 148.7 %while.30 = (s32[]{:T(128)}, f32[512,2048]{1,0:T(8,128)}, f32[16,2,512,256]{2,3,1,0:T(8,128)}, f32[16,512]{1,0:T(8,128)S(1)}, bf16[16,2,2048,256]{3,2,1,0:T(8,12...) while((s32[]{:T(128)}, f32[512,2048]{1,0:T(8,128)}, ...), condition=%wide.region_13.14_spmd.clone, body=%wide.region_12.13_spmd.clone.sunk | while | flops 1613627392 | bytes 50338988 | solution.py:157
  860.2 504.8 %while.31 = (s32[]{:T(128)}, f32[512,2048]{1,0:T(8,128)}, f32[16,2,2048,256]{3,2,1,0:T(8,128)}, f32[16,2048,256]{2,1,0:T(8,128)}, f32[16,512]{1,0:T(8,128)S(1)},...) while((s32[]{:T(128)}, f32[512,2048]{1,0:T(8,128)}, ...), condition=%wide.region_17.18_spmd.clone, body=%wide.region_15.17_spmd.clone.sunk | while | flops 3226992128 | bytes 86523664 | solution.py:192
  900.5 6.2 bitcast_add_fusion.3
  932.1 6.2 bitcast_add_fusion.3
  963.7 6.2 bitcast_add_fusion.3
  995.4 6.2 bitcast_add_fusion.3
  1027.0 6.2 bitcast_add_fusion.3
  1058.6 6.2 bitcast_add_fusion.3
  1090.2 6.2 bitcast_add_fusion.3
  1121.9 6.2 bitcast_add_fusion.3
  1153.5 6.2 bitcast_add_fusion.3
  1185.1 6.2 bitcast_add_fusion.3
  1216.7 6.2 bitcast_add_fusion.3
  1248.4 6.2 bitcast_add_fusion.3
  1280.0 6.2 bitcast_add_fusion.3
  1311.6 6.2 bitcast_add_fusion.3
  1343.2 6.2 bitcast_add_fusion.3
  1368.9 21.6 psum.67
  1390.6 130.5 %all-reduce.8.cloned.1.call-done = f32[512,2048]{1,0:T(8,128)} async-done(((f32[512,2048]{1,0:T(8,128)}), f32[512,2048]{1,0:T(8,128)}) %all-reduce.8.cloned.1.call-update) | async-done | bytes 4194320 | tf_op jit(solution)/shard_map/psum | solution.py:195
  1521.1 7.4 multiply_reduce_fusion.2
  1528.6 81.2 %all-reduce.6.cloned.1.call-done = bf16[512,2048]{1,0:T(8,128)(2,1)} async-done(((bf16[512,2048]{1,0:T(8,128)(2,1)}), bf16[512,2048]{1,0:T(8,128)(2,1)}) %all-reduce.6.cloned.1.call-update) | async-done | bytes 2097168 | tf_op jit(solution)/shard_map/psum | solution.py:160
  1609.7 7.4 multiply_add_fusion
  1620.8 7.0 fusion.48
  1649.8 21.7 reduce-scatter.13.cloned.1.call-done
  1676.3 42.4 %reduce-scatter.11.cloned.1.call-done = f32[2,256,4,128]{3,1,2,0:T(8,128)} async-done(((f32[2,1024,4,128]{3,1,2,0:T(8,128)}), f32[2,256,4,128]{3,1,2,0:T(8,128)}) %reduce-scatter.11.cloned.1.call-update) | async-done | bytes 1048592 | tf_op jit(solution)/shard_map/reduce_scatter | solution.py:244
  1736.7 19.0 all-reduce
  1759.0 7.8 convolution_bitcast_fusion.4
  1766.9 152.3 %all-reduce.10.cloned.1.call-done = f32[512,2048]{1,0:T(8,128)} async-done(((f32[512,2048]{1,0:T(8,128)}), f32[512,2048]{1,0:T(8,128)}) %all-reduce.10.cloned.1.call-update) | async-done | bytes 4194320 | tf_op jit(solution)/shard_map/psum | solution.py:274
  1924.9 9.8 convolution_bitcast_fusion.3
  1943.6 5.9 fusion.41
  1949.5 10.3 reduce-scatter.25.cloned.1.call-done
  1961.4 94.6 %reduce-scatter.15.cloned.1.call-done = f32[3,256,512]{1,2,0:T(8,128)} async-done(((f32[3,2048,512]{1,2,0:T(8,128)}), f32[3,256,512]{1,2,0:T(8,128)}) %reduce-scatter.15.cloned.1.call-update) | async-done | bytes 1572880 | tf_op jit(solution)/shard_map/reduce_scatter | solution.py:283
  2059.0 34.1 %reduce-scatter.19.cloned.1.call-done = f32[256,16]{0,1:T(8,128)} async-done(((f32[2048,16]{0,1:T(8,128)}), f32[256,16]{0,1:T(8,128)}) %reduce-scatter.19.cloned.1.call-update) | async-done | bytes 16400 | tf_op jit(solution)/shard_map/reduce_scatter | solution.py:205
  2093.0 55.1 %reduce-scatter.17.cloned.1.call-done = f32[256,512]{1,0:T(8,128)} async-done(((f32[2048,512]{1,0:T(8,128)}), f32[256,512]{1,0:T(8,128)}) %reduce-scatter.17.cloned.1.call-update) | async-done | bytes 524304 | tf_op jit(solution)/shard_map/reduce_scatter | solution.py:284
  2148.2 209.7 %reduce-scatter.23.cloned.1.call-done = f32[16,256,256]{2,1,0:T(8,128)} async-done(((f32[16,2048,256]{2,1,0:T(8,128)}), f32[16,256,256]{2,1,0:T(8,128)}) %reduce-scatter.23.cloned.1.call-update) | async-done | bytes 4194320 | tf_op jit(solution)/shard_map/reduce_scatter | solution.py:204
  2357.9 387.8 %reduce-scatter.21.cloned.1.call-done = f32[16,2,256,256]{3,2,1,0:T(8,128)} async-done(((f32[16,2,2048,256]{3,2,1,0:T(8,128)}), f32[16,2,256,256]{3,2,1,0:T(8,128)}) %reduce-scatter.21.cloned.1.call-update) | async-done | bytes 8388624 | tf_op jit(solution)/shard_map/reduce_scatter | solution.py:203
  (552 shorter events, 691.6 us)
Async XLA Ops:
  7.2 15.7 copy-start.6
  7.2 4.7 copy-start.43
  7.2 52.7 %all-gather.9.cloned.1.call-start = ((), (), s32[]{:S(2)}) async-start(), calls=%async_computation.8 | async-start | bytes 7077888 | tf_op jit(solution)/shard_map/all_gather | solution.py:65
  9.7 102.7 %all-gather.13.cloned.1.call-start = ((), (), s32[]{:S(2)}) async-start(), calls=%async_computation.10 | async-start | bytes 2621440 | tf_op jit(solution)/shard_map/all_gather | solution.py:100
  11.8 54.3 %copy-start.31 = (f32[1,2,2,128]{3,1,2,0:T(2,128)}, f32[1,2,2,128]{3,1,2,0:T(2,128)S(1)}, u32[]{:S(2)}) copy-start(f32[1,2,2,128]{3,1,2,0:T(2,128)S(1)} %copy.140) | copy-start | bytes 6148
  22.3 37.6 %copy-start.29 = (f32[1,2048]{1,0:T(1,128)}, f32[1,2048]{1,0:T(1,128)S(1)}, u32[]{:S(2)}) copy-start(f32[1,2048]{1,0:T(1,128)S(1)} %get-tuple-element.312) | copy-start | bytes 24580
  22.3 66.6 %copy-start.39 = (f32[1,512]{1,0:T(1,128)}, f32[1,512]{1,0:T(1,128)S(1)}, u32[]{:S(2)}) copy-start(f32[1,512]{1,0:T(1,128)S(1)} %get-tuple-element.324) | copy-start | bytes 6148
  22.3 68.0 %copy-start.37 = (f32[1,512]{1,0:T(1,128)}, f32[1,512]{1,0:T(1,128)S(1)}, u32[]{:S(2)}) copy-start(f32[1,512]{1,0:T(1,128)S(1)} %get-tuple-element.323) | copy-start | bytes 6148
  22.9 67.7 %copy-start.20 = (f32[256,64]{1,0:T(8,128)}, f32[256,64]{1,0:T(8,128)S(1)}, u32[]{:S(2)}) copy-start(f32[256,64]{1,0:T(8,128)S(1)} %get-tuple-element.314) | copy-start | bytes 196612
  22.9 67.7 %copy-start.22 = (f32[256,64]{1,0:T(8,128)}, f32[256,64]{1,0:T(8,128)S(1)}, u32[]{:S(2)}) copy-start(f32[256,64]{1,0:T(8,128)S(1)} %get-tuple-element.315) | copy-start | bytes 196612
  80.7 8.2 copy-start.33
  80.7 8.2 copy-start.35
  91.3 24.9 copy-start.15
  91.3 24.9 copy-start.17
  91.3 8.0 copy-start.44
  92.4 45.0 %all-gather.11.cloned.1.call-start = ((), (), s32[]{:S(2)}) async-start(), calls=%async_computation.9 | async-start | bytes 2621440 | tf_op jit(solution)/shard_map/all_gather | solution.py:101
  98.5 68.6 %all-gather.15.cloned.1.call-start = ((), (), s32[]{:S(2)}) async-start(), calls=%async_computation.11 | async-start | bytes 2359296 | tf_op jit(solution)/shard_map/all_gather | solution.py:66
  99.1 359.9 %all-gather.21.cloned.1.call-start = ((), (), s32[]{:S(2)}) async-start(), calls=%async_computation.24 | async-start | bytes 20971520 | tf_op jit(solution)/shard_map/all_gather | solution.py:125
  143.5 28.5 %copy-start.13 = (bf16[2,256,4,128]{3,2,1,0:T(4,128)(2,1)}, bf16[2,256,4,128]{3,2,1,0:T(4,128)(2,1)S(1)}, u32[]{:S(2)}) copy-start(bf16[2,256,4,128]{3,2,1,0:T(4,128)(2,1)S(1)} %copy.90) | copy-start | bytes 1572868
  172.0 10.5 copy-start.41
  172.0 376.8 %all-gather.19.cloned.1.call-start = ((), (), s32[]{:S(2)}) async-start(), calls=%async_computation.13 | async-start | bytes 18874368 | tf_op jit(solution)/shard_map/all_gather | solution.py:132
  172.6 538.9 %all-gather.17.cloned.1.call-start = ((), (), s32[]{:S(2)}) async-start(), calls=%async_computation.12 | async-start | bytes 37748736 | tf_op jit(solution)/shard_map/all_gather | solution.py:131
  173.4 1347.8 %all-reduce.8.cloned.1.call-start = ((), (), s32[]{:S(2)}) async-start(), calls=%async_computation.15 | async-start | bytes 8388608 | tf_op jit(solution)/shard_map/psum | solution.py:195
  469.1 4.6 copy-start.9
  795.2 4.1 copy-start.2
  1365.0 244.8 %all-reduce.6.cloned.1.call-start = ((), (), s32[]{:S(2)}) async-start(), calls=%async_computation.14 | async-start | bytes 4194304 | tf_op jit(solution)/shard_map/psum | solution.py:160
  1368.9 302.6 %reduce-scatter.13.cloned.1.call-start = ((), (), s32[]{:S(2)}) async-start(), calls=%async_computation.17 | async-start | bytes 5242880 | tf_op jit(solution)/shard_map/reduce_scatter | solution.py:245
  1609.7 9.4 copy-start.19
  1627.9 90.9 %reduce-scatter.11.cloned.1.call-start = ((), (), s32[]{:S(2)}) async-start(), calls=%async_computation.16 | async-start | bytes 5242880 | tf_op jit(solution)/shard_map/reduce_scatter | solution.py:244
  1633.4 7.7 copy-start.16
  1633.4 7.7 copy-start.18
  1645.1 73.7 %copy-start.21 = (f32[256,64]{1,0:T(8,128)S(1)}, f32[256,64]{1,0:T(8,128)}, u32[]{:S(2)}) copy-start(f32[256,64]{1,0:T(8,128)} %copy-done.20) | copy-start | bytes 196612
  1645.1 73.7 %copy-start.23 = (f32[256,64]{1,0:T(8,128)S(1)}, f32[256,64]{1,0:T(8,128)}, u32[]{:S(2)}) copy-start(f32[256,64]{1,0:T(8,128)} %copy-done.22) | copy-start | bytes 196612
  1645.1 274.1 %all-reduce.10.cloned.1.call-start = ((), (), s32[]{:S(2)}) async-start(), calls=%async_computation.18 | async-start | bytes 8388608 | tf_op jit(solution)/shard_map/psum | solution.py:274
  1726.0 8.2 copy-start.34
  1726.0 8.2 copy-start.36
  1726.0 8.2 copy-start.38
  1726.1 8.2 copy-start.40
  1766.8 152.4 %copy-start.30 = (f32[1,2048]{1,0:T(1,128)S(1)}, f32[1,2048]{1,0:T(1,128)}, u32[]{:S(2)}) copy-start(f32[1,2048]{1,0:T(1,128)} %copy-done.29) | copy-start | bytes 24580
  1766.8 152.4 %copy-start.32 = (f32[1,2,2,128]{3,1,2,0:T(2,128)S(1)}, f32[1,2,2,128]{3,1,2,0:T(2,128)}, u32[]{:S(2)}) copy-start(f32[1,2,2,128]{3,1,2,0:T(2,128)} %copy-done.31) | copy-start | bytes 6148
  1766.8 158.0 %copy-start.25 = (bf16[1,512,512]{1,2,0:T(8,128)(2,1)S(1)}, bf16[1,512,512]{1,2,0:T(8,128)(2,1)}, u32[]{:S(2)}) copy-start(bf16[1,512,512]{1,2,0:T(8,128)(2,1)} %copy-done.24) | copy-start | bytes 1572868
  1766.8 158.0 %copy-start.27 = (bf16[1,512,512]{1,2,0:T(8,128)(2,1)S(1)}, bf16[1,512,512]{1,2,0:T(8,128)(2,1)}, u32[]{:S(2)}) copy-start(bf16[1,512,512]{1,2,0:T(8,128)(2,1)} %copy-done.26) | copy-start | bytes 1572868
  1766.8 192.9 %reduce-scatter.25.cloned.1.call-start = ((), (), s32[]{:S(2)}) async-start(), calls=%async_computation.25 | async-start | bytes 1179648
  1924.6 131.4 %reduce-scatter.15.cloned.1.call-start = ((), (), s32[]{:S(2)}) async-start(), calls=%async_computation.19 | async-start | bytes 14155776 | tf_op jit(solution)/shard_map/reduce_scatter | solution.py:283
  1934.7 158.4 %reduce-scatter.19.cloned.1.call-start = ((), (), s32[]{:S(2)}) async-start(), calls=%async_computation.21 | async-start | bytes 147456 | tf_op jit(solution)/shard_map/reduce_scatter | solution.py:205
  1935.8 212.4 %reduce-scatter.17.cloned.1.call-start = ((), (), s32[]{:S(2)}) async-start(), calls=%async_computation.20 | async-start | bytes 4718592 | tf_op jit(solution)/shard_map/reduce_scatter | solution.py:284
  1941.3 416.6 %reduce-scatter.23.cloned.1.call-start = ((), (), s32[]{:S(2)}) async-start(), calls=%async_computation.23 | async-start | bytes 37748736 | tf_op jit(solution)/shard_map/reduce_scatter | solution.py:204
  1941.9 803.8 %reduce-scatter.21.cloned.1.call-start = ((), (), s32[]{:S(2)}) async-start(), calls=%async_computation.22 | async-start | bytes 75497472 | tf_op jit(solution)/shard_map/reduce_scatter | solution.py:203
  (90 other events, 265.4 us)
Sparse Core Ops, SparseCore 0:
  10.5 49.3 all-gather.8
  92.6 19.8 all-gather.12
  114.5 22.8 all-gather.10
  139.2 27.8 all-gather.14
  172.1 286.7 all-gather.20
  460.7 88.0 all-gather.18
  550.7 160.7 all-gather.16
  1365.1 155.9 all-reduce.7
  1524.2 85.5 all-reduce.5
  1628.0 43.4 reduce-scatter.12
  1674.2 44.5 reduce-scatter.10
  1766.9 152.2 all-reduce.9
  1924.7 35.0 reduce-scatter.24
  1963.5 92.3 reduce-scatter.14
  2059.7 33.3 reduce-scatter.18
  2096.8 51.3 reduce-scatter.16
  2152.6 205.2 reduce-scatter.22
  2361.9 383.7 reduce-scatter.20
